TPU v7x, 256 devices: a whole 4x4x8 slice. The times are simulated.
256 devices in a mesh: seq: 32 (over x, y, core), head: 8 (over z).
Axes of the slice: x: 4, y: 4, z: 8, core: 2. Of those that a mesh axis runs over, the one named last changes fastest.
Arguments:
- projected: bfloat16 [49152, 6912], P(('seq', 'head')), may hold values from -10 to 10
- segment_ids: int32 [49152], replicated, may hold values from 0 to 63, never falling along the last dimension, each value on 1 to 1536 neighbouring positions
- widths: int32 [64], replicated, may hold values from 16 to 64
Outputs:
- attended: bfloat16 [49152, 2304], P(('seq', 'head'))
Inputs may be any that keep to these rules, and one draw needn't show every extreme that they name: `segment_ids`: ids never fall along the sequence; each of the 64 samples covers 1 to 1536 consecutive positions and some sample covers exactly 1536.
All inputs are finite; a program needn't handle non-finite values.
Results may differ from a plain program's by a relative error of at most 0.0088.
Values may be sent and summed in bfloat16 or wider, within the bound.
No kernel may reach another device: no remote copies, remote signals or barrier semaphores. Data moves between devices by JAX's collectives and lax.ppermute only.
A program may use at most 128 MiB of HBM per device.

v0:
```python
import math
import jax
import jax.numpy as jnp
from jax import lax
from jax.sharding import PartitionSpec as P

D = 2304
HEADS = 24
masked_score = -1e30


def with_halo(shard, sides, width):
    for axis, dim in sides:
        size, length = (lax.axis_size(axis), shard.shape[dim])
        up = [(i, (i + 1) % size) for i in range(size - 1)]
        down = [(j, i) for i, j in up]
        last = lax.slice_in_dim(shard, length - width, length, axis=dim)
        first = lax.slice_in_dim(shard, 0, width, axis=dim)
        before = lax.ppermute(last, axis, up)
        after = lax.ppermute(first, axis, down)
        shard = jnp.concatenate([before, shard, after], axis=dim)
    return shard


def shortened(shard):

    def short(part):
        return part.astype(jnp.bfloat16) if part.dtype == jnp.float32 else part

    return jax.tree.map(short, shard)


def rotate(head_vals, row_pos, col_pos):
    quarter = head_vals.shape[-1] // 4
    frequency = 10000.0 ** (-jnp.arange(quarter, dtype=jnp.float32) / quarter)

    def turn(half_vals, place):
        angles = place.astype(jnp.float32)[:, None] * frequency[None, :]
        cosine = jnp.cos(angles)[:, None, :]
        sine_part = jnp.sin(angles)[:, None, :]
        first_half = half_vals[..., :quarter]
        second = half_vals[..., quarter:]
        return jnp.concatenate(
            [first_half * cosine - second * sine_part, first_half * sine_part + second * cosine],
            axis=-1,
        )

    middle = 2 * quarter
    return jnp.concatenate(
        [turn(head_vals[..., :middle], row_pos), turn(head_vals[..., middle:], col_pos)], axis=-1
    )


def starts_of(segment_ids):
    length = segment_ids.shape[0]
    indices = jnp.arange(length, dtype=jnp.int32)
    before = jnp.concatenate([jnp.full((1,), -1, jnp.int32), segment_ids[:-1]])
    return lax.cummax(jnp.where(segment_ids != before, indices, 0), axis=0)


def block_scores(q_rows, k_rows, q_ids, k_ids, scaling):
    scores = (
        lax.dot_general(
            q_rows, k_rows, (((1,), (1,)), ((), ())), preferred_element_type=jnp.float32
        )
        * scaling
    )
    same_seg = q_ids[:, None] == k_ids[None, :]
    return (jnp.where(same_seg, scores, masked_score), same_seg)


def dense_rows(q_rows, k_all, v_all, q_ids, k_ids, scaling):
    scores, same_seg = block_scores(q_rows, k_all, q_ids, k_ids, scaling)
    row_max = jnp.max(scores, axis=1, keepdims=True)
    weights = jnp.where(same_seg, jnp.exp(scores - row_max), 0.0)
    totals = jnp.sum(weights, axis=1, keepdims=True)
    blended = jnp.dot(weights.astype(jnp.bfloat16), v_all, preferred_element_type=jnp.float32)
    return (blended / totals).astype(jnp.bfloat16)


def attend(queries, key_rows, values, query_seg, key_seg):
    shard_rows, head_count, head_size = queries.shape
    block_rows = min(512, shard_rows)
    scaling = 1.0 / math.sqrt(head_size)

    def one_block(number):
        start_row = number * block_rows
        q_blk = lax.dynamic_slice_in_dim(queries, start_row, block_rows, 0)
        q_ids = lax.dynamic_slice_in_dim(query_seg, start_row, block_rows, 0)
        outputs = []
        for head_num in range(head_count):
            outputs.append(
                dense_rows(
                    q_blk[:, head_num],
                    key_rows[:, head_num],
                    values[:, head_num],
                    q_ids,
                    key_seg,
                    scaling,
                )
            )
        return jnp.stack(outputs, axis=1)

    results = lax.map(one_block, jnp.arange(shard_rows // block_rows, dtype=jnp.int32))
    return results.reshape(shard_rows, head_count, head_size)


def body(projected, segment_ids, widths):
    tok_dev = projected.shape[0]
    group_size = lax.axis_size("head")
    shard_rows = tok_dev * group_size
    head_size = D // HEADS
    local_heads = HEADS // group_size
    seq_index = lax.axis_index("seq")
    head_index = lax.axis_index("head")
    first_tok = (seq_index * group_size + head_index) * tok_dev
    starts = starts_of(segment_ids)
    own_seg = lax.dynamic_slice_in_dim(segment_ids, first_tok, tok_dev, 0)
    own_start = lax.dynamic_slice_in_dim(starts, first_tok, tok_dev, 0)
    offset = first_tok + jnp.arange(tok_dev, dtype=jnp.int32) - own_start
    sample_ids = jnp.arange(widths.shape[0], dtype=jnp.int32)
    width_tok = jnp.sum(
        jnp.where(own_seg[:, None] == sample_ids[None, :], widths[None, :], 0), axis=1
    )
    row_pos = offset // width_tok
    col_pos = offset % width_tok
    qkv_parts = projected.reshape(tok_dev, 3, HEADS, head_size)
    q_rot = rotate(qkv_parts[:, 0].astype(jnp.float32), row_pos, col_pos).astype(jnp.bfloat16)
    k_rot = rotate(qkv_parts[:, 1].astype(jnp.float32), row_pos, col_pos).astype(jnp.bfloat16)
    stacked = jnp.stack([q_rot, k_rot, qkv_parts[:, 2]], axis=1)
    stacked = stacked.reshape(tok_dev, 3, group_size, local_heads, head_size)
    query_seg = lax.dynamic_slice_in_dim(segment_ids, seq_index * shard_rows, shard_rows, 0)
    no_sample = jnp.full((shard_rows,), -1, jnp.int32)
    seg_pad = jnp.concatenate([no_sample, segment_ids, no_sample], axis=0)
    key_seg = lax.dynamic_slice_in_dim(seg_pad, seq_index * shard_rows, 3 * shard_rows, 0)
    qkv_part = lax.all_to_all(stacked, "head", split_axis=2, concat_axis=0, tiled=True)
    key_value = qkv_part[:, 1:]
    widened = with_halo(key_value, (("seq", 0),), qkv_part.shape[0])
    attended_heads = attend(
        qkv_part[:, 0, 0], widened[:, 0, 0], widened[:, 1, 0], query_seg, key_seg
    )
    returned = lax.all_to_all(
        shortened(attended_heads), "head", split_axis=0, concat_axis=1, tiled=True
    ).astype(attended_heads.dtype)
    return returned.reshape(tok_dev, HEADS * head_size)


def solution(mesh):
    in_specs = (P(("seq", "head"), None), P(), P())
    out_specs = P(("seq", "head"), None)
    return jax.shard_map(body, mesh=mesh, in_specs=in_specs, out_specs=out_specs, check_vma=False)
```

profile of v0, /device:TPU:6, one launch (start us, length us, event | category | flops | bytes accessed | tf_op | source)
XLA Modules:
  0.0 286.2 jit_solution(3814066336356876828)
XLA Ops:
  3.8 4.8 %copy.34 = bf16[192,6912]{0,1:T(8,128)(2,1)S(1)} copy(bf16[192,6912]{1,0:T(8,128)(2,1)} %param.5) | data formatting | bytes 5308416 | tf_op args[0]
  12.1 90.4 %all_to_all.33 = bf16[192,3,8,3,96]{0,4,3,1,2:T(8,128)(2,1)S(1)} all-to-all(bf16[192,3,8,3,96]{0,4,3,1,2:T(8,128)(2,1)S(1)} %copy.39), channel_id=1, replica_groups=mesh['seq'=32,'head'=8] {'head'}, dimensions={2} | all-to-all | bytes 5308416 | tf_op jit(solution)/shard_map/all_to_all | solution.py:136
  102.5 2.2 copy.40
  104.7 4.1 %all_to_all.27 = bf16[1536,3,1,3,96]{0,4,3,1,2:T(8,128)(2,1)} reshape(bf16[8,192,3,1,3,96]{1,0,5,4,2,3:T(8,128)(2,1)S(1)} %copy.40) | data formatting | bytes 5308416 | tf_op jit(solution)/shard_map/all_to_all | solution.py:136
  110.4 1.9 collective-permute-start
  112.3 5.8 %collective-permute-start.1 = (bf16[1536,2,1,3,96]{0,4,3,1,2:T(8,128)(2,1)S(1)}, bf16[1536,2,1,3,96]{0,4,3,1,2:T(8,128)(2,1)}, u32[]{:S(2)}, u32[]{:S(2)}) collective-permute-start(bf16[1536,2,1,3,96]{0,4,3,1,2:T(8,128)(2,1)S(1)} %slice.133), channel_id=1, source_target_pairs={{8,0},{16,8},{24,16},{32,24},{40,32},{48,40},{56,48},{64,56},{72,6... | collective-permute-start | bytes 5308424 | tf_op jit(solution)/shard_map/ppermute | solution.py:20
  120.3 2.2 slice_bitcast_fusion.4
  122.5 13.8 %collective-permute-done = bf16[1536,2,1,3,96]{0,4,3,1,2:T(8,128)(2,1)S(1)} collective-permute-done((bf16[1536,2,1,3,96]{0,4,3,1,2:T(8,128)(2,1)S(1)}, bf16[1536,2,1,3,96]{0,4,3,1,2:T(8,128)(2,1)S(1)}, u32[]{:S(2)}, u32[]{:S(2)}) %collective-permute-start) | collective-permute-done | bytes 1769504 | tf_op jit(solution)/shard_map/ppermute | solution.py:19
  138.1 2.4 pad_maximum_fusion
  142.3 97.8 %while.10 = (s32[]{:T(128)}, bf16[3,512,3,96]{1,3,2,0:T(8,128)(2,1)S(1)}, s32[3]{0:T(128)S(1)}, s32[1536]{0:T(1024)S(1)}, s32[4608]{0:T(1024)}, /*index=5*/bf16[...) while((s32[]{:T(128)}, ...), condition=%wide.region_11.12_spmd, body=%wide.region_4.11_spmd.sunk | while | flops 2799301632 | bytes 157868512 | solution.py:104
  143.8 6.4 %fusion.89 = (f32[512]{0:T(512)S(1)}, f32[512,4608]{1,0:T(8,128)}) fusion(bf16[4608,3,96]{0,2,1:T(8,128)(2,1)} %get-tuple-element.199, bf16[1536,3,96]{0,2,1:T(8,128)(2,1)} %get-tuple-element.198, s32[]{:T(128)S(6)} %select_n.123, s32[]{:T(128)S(6)} %add.94, s32[4608]{0:T(1024)} %get-tuple-element.197, s32[512]{0:T(512)S(1)} %dynamic_slice.48), kind=kOutput, calls=%fused_computation.91.clone.1 | convolution fusion | flops 462421504 | bytes 10444808 | tf_op jit(solution)/shard_map/while/body/eval_jaxpr/dot_general | solution.py:63
  150.2 6.5 %fusion.88 = (f32[512]{0:T(512)S(1)}, f32[512,4608]{1,0:T(8,128)}) fusion(bf16[4608,3,96]{0,2,1:T(8,128)(2,1)} %get-tuple-element.199, bf16[1536,3,96]{0,2,1:T(8,128)(2,1)} %get-tuple-element.198, s32[]{:T(128)S(6)} %select_n.123, s32[4608]{0:T(1024)S(1)} %copy-done.2, s32[512]{0:T(512)S(1)} %dynamic_slice.48), kind=kOutput, calls=%fused_computation.90.clone.1 | convolution fusion | flops 462421504 | bytes 10442756 | tf_op jit(solution)/shard_map/while/body/eval_jaxpr/dot_general | solution.py:63
  156.8 3.0 %fusion.87 = (f32[512]{0:T(512)S(1)}, f32[512,4608]{1,0:T(8,128)S(1)}) fusion(bf16[4608,3,96]{0,2,1:T(8,128)(2,1)} %get-tuple-element.199, bf16[1536,3,96]{0,2,1:T(8,128)(2,1)} %get-tuple-element.198, s32[]{:T(128)S(6)} %select_n.123, s32[]{:T(128)S(6)} %add.93, s32[4608]{0:T(1024)} %get-tuple-element.197, s32[512]{0:T(512)S(1)} %dynamic_slice.48), kind=kOutput, calls=%fused_computation.89.clone.1 | convolution fusion | flops 462421504 | bytes 10444808 | tf_op jit(solution)/shard_map/while/body/eval_jaxpr/dot_general | solution.py:63
  160.8 8.5 %fusion.90 = (f32[512]{0:T(512)S(1)}, f32[512]{0:T(512)S(1)}, f32[512]{0:T(512)S(1)}) fusion(f32[512,4608]{1,0:T(8,128)S(1)} %copy-done, f32[512]{0:T(512)S(1)} %get-tuple-element.159, s32[4608]{0:T(1024)S(1)} %copy-done.3, s32[512]{0:T(512)S(1)} %dynamic_slice.48, f32[512,4608]{1,0:T(8,128)} %get-tuple-element.160, f32[512]{0:T(512)S(1)} %get-tuple-element.161, ...), kind=kLoop, calls=%fused_computation.6.clone.1 | loop fusion | flops 23591424 | bytes 28344320 | tf_op jit(solution)/shard_map/while/body/eval_jaxpr/reduce_sum | solution.py:76
  169.3 1.8 fusion.93
  171.2 1.8 fusion.92
  173.0 1.8 fusion.91
  176.4 6.5 %fusion.89 = (f32[512]{0:T(512)S(1)}, f32[512,4608]{1,0:T(8,128)}) fusion(bf16[4608,3,96]{0,2,1:T(8,128)(2,1)} %get-tuple-element.199, bf16[1536,3,96]{0,2,1:T(8,128)(2,1)} %get-tuple-element.198, s32[]{:T(128)S(6)} %select_n.123, s32[]{:T(128)S(6)} %add.94, s32[4608]{0:T(1024)} %get-tuple-element.197, s32[512]{0:T(512)S(1)} %dynamic_slice.48), kind=kOutput, calls=%fused_computation.91.clone.1 | convolution fusion | flops 462421504 | bytes 10444808 | tf_op jit(solution)/shard_map/while/body/eval_jaxpr/dot_general | solution.py:63
  182.9 6.5 %fusion.88 = (f32[512]{0:T(512)S(1)}, f32[512,4608]{1,0:T(8,128)}) fusion(bf16[4608,3,96]{0,2,1:T(8,128)(2,1)} %get-tuple-element.199, bf16[1536,3,96]{0,2,1:T(8,128)(2,1)} %get-tuple-element.198, s32[]{:T(128)S(6)} %select_n.123, s32[4608]{0:T(1024)S(1)} %copy-done.2, s32[512]{0:T(512)S(1)} %dynamic_slice.48), kind=kOutput, calls=%fused_computation.90.clone.1 | convolution fusion | flops 462421504 | bytes 10442756 | tf_op jit(solution)/shard_map/while/body/eval_jaxpr/dot_general | solution.py:63
  189.4 3.0 %fusion.87 = (f32[512]{0:T(512)S(1)}, f32[512,4608]{1,0:T(8,128)S(1)}) fusion(bf16[4608,3,96]{0,2,1:T(8,128)(2,1)} %get-tuple-element.199, bf16[1536,3,96]{0,2,1:T(8,128)(2,1)} %get-tuple-element.198, s32[]{:T(128)S(6)} %select_n.123, s32[]{:T(128)S(6)} %add.93, s32[4608]{0:T(1024)} %get-tuple-element.197, s32[512]{0:T(512)S(1)} %dynamic_slice.48), kind=kOutput, calls=%fused_computation.89.clone.1 | convolution fusion | flops 462421504 | bytes 10444808 | tf_op jit(solution)/shard_map/while/body/eval_jaxpr/dot_general | solution.py:63
  193.4 8.5 %fusion.90 = (f32[512]{0:T(512)S(1)}, f32[512]{0:T(512)S(1)}, f32[512]{0:T(512)S(1)}) fusion(f32[512,4608]{1,0:T(8,128)S(1)} %copy-done, f32[512]{0:T(512)S(1)} %get-tuple-element.159, s32[4608]{0:T(1024)S(1)} %copy-done.3, s32[512]{0:T(512)S(1)} %dynamic_slice.48, f32[512,4608]{1,0:T(8,128)} %get-tuple-element.160, f32[512]{0:T(512)S(1)} %get-tuple-element.161, ...), kind=kLoop, calls=%fused_computation.6.clone.1 | loop fusion | flops 23591424 | bytes 28344320 | tf_op jit(solution)/shard_map/while/body/eval_jaxpr/reduce_sum | solution.py:76
  201.9 1.8 fusion.93
  203.8 1.8 fusion.92
  205.7 1.8 fusion.91
  209.0 6.5 %fusion.89 = (f32[512]{0:T(512)S(1)}, f32[512,4608]{1,0:T(8,128)}) fusion(bf16[4608,3,96]{0,2,1:T(8,128)(2,1)} %get-tuple-element.199, bf16[1536,3,96]{0,2,1:T(8,128)(2,1)} %get-tuple-element.198, s32[]{:T(128)S(6)} %select_n.123, s32[]{:T(128)S(6)} %add.94, s32[4608]{0:T(1024)} %get-tuple-element.197, s32[512]{0:T(512)S(1)} %dynamic_slice.48), kind=kOutput, calls=%fused_computation.91.clone.1 | convolution fusion | flops 462421504 | bytes 10444808 | tf_op jit(solution)/shard_map/while/body/eval_jaxpr/dot_general | solution.py:63
  215.5 6.5 %fusion.88 = (f32[512]{0:T(512)S(1)}, f32[512,4608]{1,0:T(8,128)}) fusion(bf16[4608,3,96]{0,2,1:T(8,128)(2,1)} %get-tuple-element.199, bf16[1536,3,96]{0,2,1:T(8,128)(2,1)} %get-tuple-element.198, s32[]{:T(128)S(6)} %select_n.123, s32[4608]{0:T(1024)S(1)} %copy-done.2, s32[512]{0:T(512)S(1)} %dynamic_slice.48), kind=kOutput, calls=%fused_computation.90.clone.1 | convolution fusion | flops 462421504 | bytes 10442756 | tf_op jit(solution)/shard_map/while/body/eval_jaxpr/dot_general | solution.py:63
  222.0 3.0 %fusion.87 = (f32[512]{0:T(512)S(1)}, f32[512,4608]{1,0:T(8,128)S(1)}) fusion(bf16[4608,3,96]{0,2,1:T(8,128)(2,1)} %get-tuple-element.199, bf16[1536,3,96]{0,2,1:T(8,128)(2,1)} %get-tuple-element.198, s32[]{:T(128)S(6)} %select_n.123, s32[]{:T(128)S(6)} %add.93, s32[4608]{0:T(1024)} %get-tuple-element.197, s32[512]{0:T(512)S(1)} %dynamic_slice.48), kind=kOutput, calls=%fused_computation.89.clone.1 | convolution fusion | flops 462421504 | bytes 10444808 | tf_op jit(solution)/shard_map/while/body/eval_jaxpr/dot_general | solution.py:63
  226.0 8.5 %fusion.90 = (f32[512]{0:T(512)S(1)}, f32[512]{0:T(512)S(1)}, f32[512]{0:T(512)S(1)}) fusion(f32[512,4608]{1,0:T(8,128)S(1)} %copy-done, f32[512]{0:T(512)S(1)} %get-tuple-element.159, s32[4608]{0:T(1024)S(1)} %copy-done.3, s32[512]{0:T(512)S(1)} %dynamic_slice.48, f32[512,4608]{1,0:T(8,128)} %get-tuple-element.160, f32[512]{0:T(512)S(1)} %get-tuple-element.161, ...), kind=kLoop, calls=%fused_computation.6.clone.1 | loop fusion | flops 23591424 | bytes 28344320 | tf_op jit(solution)/shard_map/while/body/eval_jaxpr/reduce_sum | solution.py:76
  234.5 1.8 fusion.93
  236.4 1.8 fusion.92
  238.3 1.8 fusion.91
  241.2 42.7 %all_to_all.34 = bf16[1536,3,96]{2,1,0:T(4,128)(2,1)S(1)} all-to-all(bf16[1536,3,96]{2,1,0:T(4,128)(2,1)S(1)} %bitcast.128), channel_id=1, replica_groups=mesh['seq'=32,'head'=8] {'head'}, dimensions={0} | all-to-all | bytes 1769472 | tf_op jit(solution)/shard_map/all_to_all | solution.py:142
  (97 shorter events, 23.2 us)
Async XLA Ops:
  3.8 5.3 %copy-start.6 = (s32[64]{0:T(128)S(1)}, s32[64]{0:T(128)}, u32[]{:S(2)}) copy-start(s32[64]{0:T(128)} %param.7) | copy-start | bytes 772
  110.4 26.0 %collective-permute-start = (bf16[1536,2,1,3,96]{0,4,3,1,2:T(8,128)(2,1)S(1)}, bf16[1536,2,1,3,96]{0,4,3,1,2:T(8,128)(2,1)S(1)}, u32[]{:S(2)}, u32[]{:S(2)}) collective-permute-start(bf16[1536,2,1,3,96]{0,4,3,1,2:T(8,128)(2,1)S(1)} %slice.133), channel_id=1, source_target_pairs={{0,8},{8,16},{16,24},{24,32},{32,40},{40,48},{48,56},{56,64},{64,7... | collective-permute-start | bytes 5308424 | tf_op jit(solution)/shard_map/ppermute | solution.py:19
  112.3 25.8 %collective-permute-start.1 = (bf16[1536,2,1,3,96]{0,4,3,1,2:T(8,128)(2,1)S(1)}, bf16[1536,2,1,3,96]{0,4,3,1,2:T(8,128)(2,1)}, u32[]{:S(2)}, u32[]{:S(2)}) collective-permute-start(bf16[1536,2,1,3,96]{0,4,3,1,2:T(8,128)(2,1)S(1)} %slice.133), channel_id=1, source_target_pairs={{8,0},{16,8},{24,16},{32,24},{40,32},{48,40},{56,48},{64,56},{72,6... | collective-permute-start | bytes 5308424 | tf_op jit(solution)/shard_map/ppermute | solution.py:20
  140.5 1.8 copy-start.1
  142.3 1.4 copy-start.4
  143.8 6.5 %copy-start.2 = (s32[4608]{0:T(1024)S(1)}, s32[4608]{0:T(1024)}, u32[]{:S(2)}) copy-start(s32[4608]{0:T(1024)} %get-tuple-element.197) | copy-start | bytes 55300 | tf_op jit(solution)/shard_map/while
  156.8 4.0 %copy-start = (f32[512,4608]{1,0:T(8,128)S(1)}, f32[512,4608]{1,0:T(8,128)}, u32[]{:S(2)}) copy-start(f32[512,4608]{1,0:T(8,128)} %get-tuple-element.158) | copy-start | bytes 28311556 | tf_op jit(solution)/shard_map/while
  156.8 4.0 %copy-start.3 = (s32[4608]{0:T(1024)S(1)}, s32[4608]{0:T(1024)}, u32[]{:S(2)}) copy-start(s32[4608]{0:T(1024)} %get-tuple-element.197) | copy-start | bytes 55300 | tf_op jit(solution)/shard_map/while
  160.8 10.4 %slice-start = ((s8[9437184]{0:T(1024)(128)(4,1)}), s8[4194304]{0:T(1024)(128)(4,1)S(1)}, s32[]{:S(2)}) async-start(s8[9437184]{0:T(1024)(128)(4,1)} %bitcast.124), calls=%async_computation.2 | async-start | bytes 8388608 | tf_op jit(solution)/shard_map/while
  160.8 10.4 %slice-start.1 = ((s8[9437184]{0:T(1024)(128)(4,1)}), s8[4194304]{0:T(1024)(128)(4,1)S(1)}, s32[]{:S(2)}) async-start(s8[9437184]{0:T(1024)(128)(4,1)} %bitcast.124), calls=%async_computation.3 | async-start | bytes 8388608 | tf_op jit(solution)/shard_map/while
  169.3 1.9 slice-start.2
  173.0 1.9 copy-start.5
  174.9 1.5 copy-start.4
  176.4 6.5 %copy-start.2 = (s32[4608]{0:T(1024)S(1)}, s32[4608]{0:T(1024)}, u32[]{:S(2)}) copy-start(s32[4608]{0:T(1024)} %get-tuple-element.197) | copy-start | bytes 55300 | tf_op jit(solution)/shard_map/while
  189.4 4.0 %copy-start = (f32[512,4608]{1,0:T(8,128)S(1)}, f32[512,4608]{1,0:T(8,128)}, u32[]{:S(2)}) copy-start(f32[512,4608]{1,0:T(8,128)} %get-tuple-element.158) | copy-start | bytes 28311556 | tf_op jit(solution)/shard_map/while
  189.4 4.0 %copy-start.3 = (s32[4608]{0:T(1024)S(1)}, s32[4608]{0:T(1024)}, u32[]{:S(2)}) copy-start(s32[4608]{0:T(1024)} %get-tuple-element.197) | copy-start | bytes 55300 | tf_op jit(solution)/shard_map/while
  193.4 10.4 %slice-start = ((s8[9437184]{0:T(1024)(128)(4,1)}), s8[4194304]{0:T(1024)(128)(4,1)S(1)}, s32[]{:S(2)}) async-start(s8[9437184]{0:T(1024)(128)(4,1)} %bitcast.124), calls=%async_computation.2 | async-start | bytes 8388608 | tf_op jit(solution)/shard_map/while
  193.4 10.4 %slice-start.1 = ((s8[9437184]{0:T(1024)(128)(4,1)}), s8[4194304]{0:T(1024)(128)(4,1)S(1)}, s32[]{:S(2)}) async-start(s8[9437184]{0:T(1024)(128)(4,1)} %bitcast.124), calls=%async_computation.3 | async-start | bytes 8388608 | tf_op jit(solution)/shard_map/while
  201.9 1.9 slice-start.2
  205.6 1.9 copy-start.5
  207.6 1.5 copy-start.4
  209.0 6.5 %copy-start.2 = (s32[4608]{0:T(1024)S(1)}, s32[4608]{0:T(1024)}, u32[]{:S(2)}) copy-start(s32[4608]{0:T(1024)} %get-tuple-element.197) | copy-start | bytes 55300 | tf_op jit(solution)/shard_map/while
  222.0 4.0 %copy-start = (f32[512,4608]{1,0:T(8,128)S(1)}, f32[512,4608]{1,0:T(8,128)}, u32[]{:S(2)}) copy-start(f32[512,4608]{1,0:T(8,128)} %get-tuple-element.158) | copy-start | bytes 28311556 | tf_op jit(solution)/shard_map/while
  222.0 4.0 %copy-start.3 = (s32[4608]{0:T(1024)S(1)}, s32[4608]{0:T(1024)}, u32[]{:S(2)}) copy-start(s32[4608]{0:T(1024)} %get-tuple-element.197) | copy-start | bytes 55300 | tf_op jit(solution)/shard_map/while
  226.0 10.4 %slice-start = ((s8[9437184]{0:T(1024)(128)(4,1)}), s8[4194304]{0:T(1024)(128)(4,1)S(1)}, s32[]{:S(2)}) async-start(s8[9437184]{0:T(1024)(128)(4,1)} %bitcast.124), calls=%async_computation.2 | async-start | bytes 8388608 | tf_op jit(solution)/shard_map/while
  226.0 10.4 %slice-start.1 = ((s8[9437184]{0:T(1024)(128)(4,1)}), s8[4194304]{0:T(1024)(128)(4,1)S(1)}, s32[]{:S(2)}) async-start(s8[9437184]{0:T(1024)(128)(4,1)} %bitcast.124), calls=%async_computation.3 | async-start | bytes 8388608 | tf_op jit(solution)/shard_map/while
  234.5 1.9 slice-start.2
  238.3 1.9 copy-start.5
where the time goes:
time: 287 us; the launch traced here: 286 us
  blocking collectives  133 us (46%)
  matrix products  64.6 us (23%)
  other arithmetic  34.4 us (12%)
  local copies, waits for them, and re-layouts  28.2 us (10%)
  waiting for transfers between devices  15.6 us (5%)
  starting transfers between devices  7.67 us (3%)
    all_to_all x1, blocking collectives, body(): lax.all_to_all(stacked, 'head', split_axis=2, concat_axis=0, tiled=True)  90.4 us
    dot_general x9, matrix products, block_scores(): lax.dot_general(q_rows, k_rows, (((1,), (1,)), ((), ())), preferred_eleme...  48.1 us
    all_to_all x1, blocking collectives, body(): lax.all_to_all(shortened(attended_heads), 'head', split_axis=0, concat_ax...  42.7 us
    reduce_sum x3, other arithmetic, dense_rows(): totals = jnp.sum(weights, axis=1, keepdims=True)  25.5 us
    dot_general x9, matrix products, dense_rows(): jnp.dot(weights.astype(jnp.bfloat16), v_all, preferred_element_type=jnp.f...  16.5 us
    ppermute x1, waiting for transfers between devices, with_halo(): before = lax.ppermute(last, axis, up)  13.8 us
    all_to_all x2, local copies, waits for them, and re-layouts, body(): lax.all_to_all(stacked, 'head', split_axis=2, concat_axis=0, tiled=True)  6.32 us
    ppermute x1, starting transfers between devices, with_halo(): after = lax.ppermute(first, axis, down)  5.75 us
  transfers between devices with their start and end apart: 2, of which 2 were waited for; matrix products, arithmetic and copies ran while one was open for 2% of the time, Pallas kernels for 0%

commit v1 on v0

--- a/solution.py
+++ b/solution.py
@@ -139,8 +139,14 @@
     attended_heads = attend(
         qkv_part[:, 0, 0], widened[:, 0, 0], widened[:, 1, 0], query_seg, key_seg
     )
-    returned = lax.all_to_all(
-        shortened(attended_heads), "head", split_axis=0, concat_axis=1, tiled=True
+    returned = jnp.concatenate(
+        lax.all_to_all(
+            jnp.stack(jnp.split(shortened(attended_heads), lax.axis_size("head"), axis=0)),
+            "head",
+            0,
+            0,
+        ),
+        axis=1,
     ).astype(attended_heads.dtype)
     return returned.reshape(tok_dev, HEADS * head_size)
 

time: 287 us -> 276 us (0.962)
  blocking collectives: 133 us -> 125 us
    all_to_all x1, blocking collectives: 42.7 us -> 34.2 us  [body(): lax.all_to_all(jnp.stack(jnp.split(shortened(attended_heads), lax.axis_si...]
where the time goes in v1:
time: 276 us; the launch traced here: 275 us
  blocking collectives  125 us (45%)
  matrix products  64.6 us (23%)
  other arithmetic  33.4 us (12%)
  local copies, waits for them, and re-layouts  26.9 us (10%)
  waiting for transfers between devices  15.6 us (6%)
  starting transfers between devices  7.67 us (3%)
    all_to_all x1, blocking collectives, body(): lax.all_to_all(stacked, 'head', split_axis=2, concat_axis=0, tiled=True)  90.4 us
    dot_general x9, matrix products, block_scores(): lax.dot_general(q_rows, k_rows, (((1,), (1,)), ((), ())), preferred_eleme...  48.1 us
    all_to_all x1, blocking collectives, body(): lax.all_to_all(jnp.stack(jnp.split(shortened(attended_heads), lax.axis_si...  34.2 us
    reduce_sum x3, other arithmetic, dense_rows(): totals = jnp.sum(weights, axis=1, keepdims=True)  24.5 us
    dot_general x9, matrix products, dense_rows(): jnp.dot(weights.astype(jnp.bfloat16), v_all, preferred_element_type=jnp.f...  16.5 us
    ppermute x1, waiting for transfers between devices, with_halo(): before = lax.ppermute(last, axis, up)  13.8 us
    all_to_all x2, local copies, waits for them, and re-layouts, body(): lax.all_to_all(stacked, 'head', split_axis=2, concat_axis=0, tiled=True)  6.32 us
    ppermute x1, starting transfers between devices, with_halo(): after = lax.ppermute(first, axis, down)  5.75 us
  transfers between devices with their start and end apart: 2, of which 2 were waited for; matrix products, arithmetic and copies ran while one was open for 2% of the time, Pallas kernels for 0%

profile of v1, /device:TPU:6, one launch (start us, length us, event | category | flops | bytes accessed | tf_op | source)
XLA Modules:
  0.0 275.4 jit_solution(11196415709342648191)
XLA Ops:
  3.8 4.8 %copy.36 = bf16[192,6912]{0,1:T(8,128)(2,1)S(1)} copy(bf16[192,6912]{1,0:T(8,128)(2,1)} %param.5) | data formatting | bytes 5308416 | tf_op args[0]
  12.2 90.4 %all_to_all.23 = bf16[192,3,8,3,96]{0,4,3,1,2:T(8,128)(2,1)S(1)} all-to-all(bf16[192,3,8,3,96]{0,4,3,1,2:T(8,128)(2,1)S(1)} %copy.41), channel_id=1, replica_groups=mesh['seq'=32,'head'=8] {'head'}, dimensions={2} | all-to-all | bytes 5308416 | tf_op jit(solution)/shard_map/all_to_all | solution.py:136
  102.6 2.2 copy.42
  104.8 4.1 %all_to_all.19 = bf16[1536,3,1,3,96]{0,4,3,1,2:T(8,128)(2,1)} reshape(bf16[8,192,3,1,3,96]{1,0,5,4,2,3:T(8,128)(2,1)S(1)} %copy.42) | data formatting | bytes 5308416 | tf_op jit(solution)/shard_map/all_to_all | solution.py:136
  110.5 1.9 collective-permute-start
  112.4 5.8 %collective-permute-start.1 = (bf16[1536,2,1,3,96]{0,4,3,1,2:T(8,128)(2,1)S(1)}, bf16[1536,2,1,3,96]{0,4,3,1,2:T(8,128)(2,1)}, u32[]{:S(2)}, u32[]{:S(2)}) collective-permute-start(bf16[1536,2,1,3,96]{0,4,3,1,2:T(8,128)(2,1)S(1)} %slice.133), channel_id=1, source_target_pairs={{8,0},{16,8},{24,16},{32,24},{40,32},{48,40},{56,48},{64,56},{72,6... | collective-permute-start | bytes 5308424 | tf_op jit(solution)/shard_map/ppermute | solution.py:20
  120.4 2.2 slice_bitcast_fusion.4
  122.6 13.8 %collective-permute-done = bf16[1536,2,1,3,96]{0,4,3,1,2:T(8,128)(2,1)S(1)} collective-permute-done((bf16[1536,2,1,3,96]{0,4,3,1,2:T(8,128)(2,1)S(1)}, bf16[1536,2,1,3,96]{0,4,3,1,2:T(8,128)(2,1)S(1)}, u32[]{:S(2)}, u32[]{:S(2)}) %collective-permute-start) | collective-permute-done | bytes 1769504 | tf_op jit(solution)/shard_map/ppermute | solution.py:19
  138.2 2.4 pad_maximum_fusion
  142.5 96.8 %while.10 = (s32[]{:T(128)}, bf16[3,512,3,96]{1,3,2,0:T(8,128)(2,1)S(1)}, s32[3]{0:T(128)S(1)}, s32[1536]{0:T(1024)S(1)}, s32[4608]{0:T(1024)}, /*index=5*/bf16[...) while((s32[]{:T(128)}, ...), condition=%wide.region_11.12_spmd, body=%wide.region_4.11_spmd.sunk | while | flops 2799301632 | bytes 157868512 | solution.py:104
  143.9 6.5 %fusion.97 = (f32[512]{0:T(512)S(1)}, f32[512,4608]{1,0:T(8,128)}) fusion(bf16[4608,3,96]{0,2,1:T(8,128)(2,1)} %get-tuple-element.199, bf16[1536,3,96]{0,2,1:T(8,128)(2,1)} %get-tuple-element.198, s32[]{:T(128)S(6)} %select_n.123, s32[]{:T(128)S(6)} %add.94, s32[4608]{0:T(1024)} %get-tuple-element.197, s32[512]{0:T(512)S(1)} %dynamic_slice.48), kind=kOutput, calls=%fused_computation.107.clone.1 | convolution fusion | flops 462421504 | bytes 10444808 | tf_op jit(solution)/shard_map/while/body/eval_jaxpr/dot_general | solution.py:63
  150.4 6.5 %fusion.96 = (f32[512]{0:T(512)S(1)}, f32[512,4608]{1,0:T(8,128)}) fusion(bf16[4608,3,96]{0,2,1:T(8,128)(2,1)} %get-tuple-element.199, bf16[1536,3,96]{0,2,1:T(8,128)(2,1)} %get-tuple-element.198, s32[]{:T(128)S(6)} %select_n.123, s32[4608]{0:T(1024)S(1)} %copy-done.2, s32[512]{0:T(512)S(1)} %dynamic_slice.48), kind=kOutput, calls=%fused_computation.106.clone.1 | convolution fusion | flops 462421504 | bytes 10442756 | tf_op jit(solution)/shard_map/while/body/eval_jaxpr/dot_general | solution.py:63
  156.9 3.0 %fusion.95 = (f32[512]{0:T(512)S(1)}, f32[512,4608]{1,0:T(8,128)S(1)}) fusion(bf16[4608,3,96]{0,2,1:T(8,128)(2,1)} %get-tuple-element.199, bf16[1536,3,96]{0,2,1:T(8,128)(2,1)} %get-tuple-element.198, s32[]{:T(128)S(6)} %select_n.123, s32[]{:T(128)S(6)} %add.93, s32[4608]{0:T(1024)} %get-tuple-element.197, s32[512]{0:T(512)S(1)} %dynamic_slice.48), kind=kOutput, calls=%fused_computation.105.clone.1 | convolution fusion | flops 462421504 | bytes 10444808 | tf_op jit(solution)/shard_map/while/body/eval_jaxpr/dot_general | solution.py:63
  160.9 8.2 %fusion.98 = (f32[512]{0:T(512)S(1)}, f32[512]{0:T(512)S(1)}, f32[512]{0:T(512)S(1)}) fusion(f32[512,4608]{1,0:T(8,128)} %get-tuple-element.158, f32[512]{0:T(512)S(1)} %get-tuple-element.159, s32[4608]{0:T(1024)} %get-tuple-element.197, s32[512]{0:T(512)S(1)} %dynamic_slice.48, f32[512,4608]{1,0:T(8,128)S(1)} %copy-done, ...), kind=kLoop, calls=%fused_computation.6.clone.1 | loop fusion | flops 23591424 | bytes 28344320 | tf_op jit(solution)/shard_map/while/body/eval_jaxpr/reduce_sum | solution.py:76
  169.1 1.8 fusion.101
  171.0 1.8 fusion.100
  172.8 1.8 fusion.99
  176.2 6.5 %fusion.97 = (f32[512]{0:T(512)S(1)}, f32[512,4608]{1,0:T(8,128)}) fusion(bf16[4608,3,96]{0,2,1:T(8,128)(2,1)} %get-tuple-element.199, bf16[1536,3,96]{0,2,1:T(8,128)(2,1)} %get-tuple-element.198, s32[]{:T(128)S(6)} %select_n.123, s32[]{:T(128)S(6)} %add.94, s32[4608]{0:T(1024)} %get-tuple-element.197, s32[512]{0:T(512)S(1)} %dynamic_slice.48), kind=kOutput, calls=%fused_computation.107.clone.1 | convolution fusion | flops 462421504 | bytes 10444808 | tf_op jit(solution)/shard_map/while/body/eval_jaxpr/dot_general | solution.py:63
  182.7 6.5 %fusion.96 = (f32[512]{0:T(512)S(1)}, f32[512,4608]{1,0:T(8,128)}) fusion(bf16[4608,3,96]{0,2,1:T(8,128)(2,1)} %get-tuple-element.199, bf16[1536,3,96]{0,2,1:T(8,128)(2,1)} %get-tuple-element.198, s32[]{:T(128)S(6)} %select_n.123, s32[4608]{0:T(1024)S(1)} %copy-done.2, s32[512]{0:T(512)S(1)} %dynamic_slice.48), kind=kOutput, calls=%fused_computation.106.clone.1 | convolution fusion | flops 462421504 | bytes 10442756 | tf_op jit(solution)/shard_map/while/body/eval_jaxpr/dot_general | solution.py:63
  189.2 3.0 %fusion.95 = (f32[512]{0:T(512)S(1)}, f32[512,4608]{1,0:T(8,128)S(1)}) fusion(bf16[4608,3,96]{0,2,1:T(8,128)(2,1)} %get-tuple-element.199, bf16[1536,3,96]{0,2,1:T(8,128)(2,1)} %get-tuple-element.198, s32[]{:T(128)S(6)} %select_n.123, s32[]{:T(128)S(6)} %add.93, s32[4608]{0:T(1024)} %get-tuple-element.197, s32[512]{0:T(512)S(1)} %dynamic_slice.48), kind=kOutput, calls=%fused_computation.105.clone.1 | convolution fusion | flops 462421504 | bytes 10444808 | tf_op jit(solution)/shard_map/while/body/eval_jaxpr/dot_general | solution.py:63
  193.2 8.2 %fusion.98 = (f32[512]{0:T(512)S(1)}, f32[512]{0:T(512)S(1)}, f32[512]{0:T(512)S(1)}) fusion(f32[512,4608]{1,0:T(8,128)} %get-tuple-element.158, f32[512]{0:T(512)S(1)} %get-tuple-element.159, s32[4608]{0:T(1024)} %get-tuple-element.197, s32[512]{0:T(512)S(1)} %dynamic_slice.48, f32[512,4608]{1,0:T(8,128)S(1)} %copy-done, ...), kind=kLoop, calls=%fused_computation.6.clone.1 | loop fusion | flops 23591424 | bytes 28344320 | tf_op jit(solution)/shard_map/while/body/eval_jaxpr/reduce_sum | solution.py:76
  201.4 1.8 fusion.101
  203.2 1.8 fusion.100
  205.1 1.8 fusion.99
  208.4 6.5 %fusion.97 = (f32[512]{0:T(512)S(1)}, f32[512,4608]{1,0:T(8,128)}) fusion(bf16[4608,3,96]{0,2,1:T(8,128)(2,1)} %get-tuple-element.199, bf16[1536,3,96]{0,2,1:T(8,128)(2,1)} %get-tuple-element.198, s32[]{:T(128)S(6)} %select_n.123, s32[]{:T(128)S(6)} %add.94, s32[4608]{0:T(1024)} %get-tuple-element.197, s32[512]{0:T(512)S(1)} %dynamic_slice.48), kind=kOutput, calls=%fused_computation.107.clone.1 | convolution fusion | flops 462421504 | bytes 10444808 | tf_op jit(solution)/shard_map/while/body/eval_jaxpr/dot_general | solution.py:63
  214.9 6.5 %fusion.96 = (f32[512]{0:T(512)S(1)}, f32[512,4608]{1,0:T(8,128)}) fusion(bf16[4608,3,96]{0,2,1:T(8,128)(2,1)} %get-tuple-element.199, bf16[1536,3,96]{0,2,1:T(8,128)(2,1)} %get-tuple-element.198, s32[]{:T(128)S(6)} %select_n.123, s32[4608]{0:T(1024)S(1)} %copy-done.2, s32[512]{0:T(512)S(1)} %dynamic_slice.48), kind=kOutput, calls=%fused_computation.106.clone.1 | convolution fusion | flops 462421504 | bytes 10442756 | tf_op jit(solution)/shard_map/while/body/eval_jaxpr/dot_general | solution.py:63
  221.4 3.0 %fusion.95 = (f32[512]{0:T(512)S(1)}, f32[512,4608]{1,0:T(8,128)S(1)}) fusion(bf16[4608,3,96]{0,2,1:T(8,128)(2,1)} %get-tuple-element.199, bf16[1536,3,96]{0,2,1:T(8,128)(2,1)} %get-tuple-element.198, s32[]{:T(128)S(6)} %select_n.123, s32[]{:T(128)S(6)} %add.93, s32[4608]{0:T(1024)} %get-tuple-element.197, s32[512]{0:T(512)S(1)} %dynamic_slice.48), kind=kOutput, calls=%fused_computation.105.clone.1 | convolution fusion | flops 462421504 | bytes 10444808 | tf_op jit(solution)/shard_map/while/body/eval_jaxpr/dot_general | solution.py:63
  225.4 8.2 %fusion.98 = (f32[512]{0:T(512)S(1)}, f32[512]{0:T(512)S(1)}, f32[512]{0:T(512)S(1)}) fusion(f32[512,4608]{1,0:T(8,128)} %get-tuple-element.158, f32[512]{0:T(512)S(1)} %get-tuple-element.159, s32[4608]{0:T(1024)} %get-tuple-element.197, s32[512]{0:T(512)S(1)} %dynamic_slice.48, f32[512,4608]{1,0:T(8,128)S(1)} %copy-done, ...), kind=kLoop, calls=%fused_computation.6.clone.1 | loop fusion | flops 23591424 | bytes 28344320 | tf_op jit(solution)/shard_map/while/body/eval_jaxpr/reduce_sum | solution.py:76
  233.7 1.8 fusion.101
  235.5 1.8 fusion.100
  237.4 1.8 fusion.99
  239.9 34.2 %all_to_all.24 = bf16[8,192,3,96]{1,3,2,0:T(8,128)(2,1)S(1)} all-to-all(bf16[8,192,3,96]{1,3,2,0:T(8,128)(2,1)S(1)} %fusion.60), channel_id=1, replica_groups=mesh['seq'=32,'head'=8] {'head'}, dimensions={0} | all-to-all | bytes 1769472 | tf_op jit(solution)/shard_map/all_to_all | solution.py:143
  (104 shorter events, 21.9 us)
Async XLA Ops:
  8.6 0.7 copy-start.6
  110.5 26.0 %collective-permute-start = (bf16[1536,2,1,3,96]{0,4,3,1,2:T(8,128)(2,1)S(1)}, bf16[1536,2,1,3,96]{0,4,3,1,2:T(8,128)(2,1)S(1)}, u32[]{:S(2)}, u32[]{:S(2)}) collective-permute-start(bf16[1536,2,1,3,96]{0,4,3,1,2:T(8,128)(2,1)S(1)} %slice.133), channel_id=1, source_target_pairs={{0,8},{8,16},{16,24},{24,32},{32,40},{40,48},{48,56},{56,64},{64,7... | collective-permute-start | bytes 5308424 | tf_op jit(solution)/shard_map/ppermute | solution.py:19
  112.4 25.8 %collective-permute-start.1 = (bf16[1536,2,1,3,96]{0,4,3,1,2:T(8,128)(2,1)S(1)}, bf16[1536,2,1,3,96]{0,4,3,1,2:T(8,128)(2,1)}, u32[]{:S(2)}, u32[]{:S(2)}) collective-permute-start(bf16[1536,2,1,3,96]{0,4,3,1,2:T(8,128)(2,1)S(1)} %slice.133), channel_id=1, source_target_pairs={{8,0},{16,8},{24,16},{32,24},{40,32},{48,40},{56,48},{64,56},{72,6... | collective-permute-start | bytes 5308424 | tf_op jit(solution)/shard_map/ppermute | solution.py:20
  140.6 1.8 copy-start.1
  142.5 1.4 copy-start.4
  143.9 6.5 %copy-start.2 = (s32[4608]{0:T(1024)S(1)}, s32[4608]{0:T(1024)}, u32[]{:S(2)}) copy-start(s32[4608]{0:T(1024)} %get-tuple-element.197) | copy-start | bytes 55300 | tf_op jit(solution)/shard_map/while
  156.9 4.0 %copy-start = (f32[512,4608]{1,0:T(8,128)S(1)}, f32[512,4608]{1,0:T(8,128)}, u32[]{:S(2)}) copy-start(f32[512,4608]{1,0:T(8,128)} %get-tuple-element.160) | copy-start | bytes 28311556 | tf_op jit(solution)/shard_map/while
  156.9 12.2 %slice-start = ((s8[9437184]{0:T(1024)(128)(4,1)}), s8[4194304]{0:T(1024)(128)(4,1)S(1)}, s32[]{:S(2)}) async-start(s8[9437184]{0:T(1024)(128)(4,1)} %bitcast.155), calls=%async_computation.2 | async-start | bytes 8388608 | tf_op jit(solution)/shard_map/while
  160.9 8.2 %slice-start.1 = ((s8[9437184]{0:T(1024)(128)(4,1)}), s8[4194304]{0:T(1024)(128)(4,1)S(1)}, s32[]{:S(2)}) async-start(s8[9437184]{0:T(1024)(128)(4,1)} %bitcast.155), calls=%async_computation.3 | async-start | bytes 8388608 | tf_op jit(solution)/shard_map/while
  160.9 8.2 %slice-start.2 = ((s8[9437184]{0:T(1024)(128)(4,1)}), s8[1048576]{0:T(1024)(128)(4,1)S(1)}, s32[]{:S(2)}) async-start(s8[9437184]{0:T(1024)(128)(4,1)} %bitcast.155), calls=%async_computation.4 | async-start | bytes 2097152 | tf_op jit(solution)/shard_map/while
  160.9 8.2 %copy-start.3 = (s32[4608]{0:T(1024)S(1)}, s32[4608]{0:T(1024)}, u32[]{:S(2)}) copy-start(s32[4608]{0:T(1024)} %get-tuple-element.197) | copy-start | bytes 55300 | tf_op jit(solution)/shard_map/while
  172.8 1.9 copy-start.5
  174.7 1.5 copy-start.4
  176.2 6.5 %copy-start.2 = (s32[4608]{0:T(1024)S(1)}, s32[4608]{0:T(1024)}, u32[]{:S(2)}) copy-start(s32[4608]{0:T(1024)} %get-tuple-element.197) | copy-start | bytes 55300 | tf_op jit(solution)/shard_map/while
  189.2 4.0 %copy-start = (f32[512,4608]{1,0:T(8,128)S(1)}, f32[512,4608]{1,0:T(8,128)}, u32[]{:S(2)}) copy-start(f32[512,4608]{1,0:T(8,128)} %get-tuple-element.160) | copy-start | bytes 28311556 | tf_op jit(solution)/shard_map/while
  189.2 12.2 %slice-start = ((s8[9437184]{0:T(1024)(128)(4,1)}), s8[4194304]{0:T(1024)(128)(4,1)S(1)}, s32[]{:S(2)}) async-start(s8[9437184]{0:T(1024)(128)(4,1)} %bitcast.155), calls=%async_computation.2 | async-start | bytes 8388608 | tf_op jit(solution)/shard_map/while
  193.2 8.2 %slice-start.1 = ((s8[9437184]{0:T(1024)(128)(4,1)}), s8[4194304]{0:T(1024)(128)(4,1)S(1)}, s32[]{:S(2)}) async-start(s8[9437184]{0:T(1024)(128)(4,1)} %bitcast.155), calls=%async_computation.3 | async-start | bytes 8388608 | tf_op jit(solution)/shard_map/while
  193.2 8.2 %slice-start.2 = ((s8[9437184]{0:T(1024)(128)(4,1)}), s8[1048576]{0:T(1024)(128)(4,1)S(1)}, s32[]{:S(2)}) async-start(s8[9437184]{0:T(1024)(128)(4,1)} %bitcast.155), calls=%async_computation.4 | async-start | bytes 2097152 | tf_op jit(solution)/shard_map/while
  193.2 8.2 %copy-start.3 = (s32[4608]{0:T(1024)S(1)}, s32[4608]{0:T(1024)}, u32[]{:S(2)}) copy-start(s32[4608]{0:T(1024)} %get-tuple-element.197) | copy-start | bytes 55300 | tf_op jit(solution)/shard_map/while
  205.1 1.9 copy-start.5
  207.0 1.5 copy-start.4
  208.4 6.5 %copy-start.2 = (s32[4608]{0:T(1024)S(1)}, s32[4608]{0:T(1024)}, u32[]{:S(2)}) copy-start(s32[4608]{0:T(1024)} %get-tuple-element.197) | copy-start | bytes 55300 | tf_op jit(solution)/shard_map/while
  221.4 4.0 %copy-start = (f32[512,4608]{1,0:T(8,128)S(1)}, f32[512,4608]{1,0:T(8,128)}, u32[]{:S(2)}) copy-start(f32[512,4608]{1,0:T(8,128)} %get-tuple-element.160) | copy-start | bytes 28311556 | tf_op jit(solution)/shard_map/while
  221.4 12.2 %slice-start = ((s8[9437184]{0:T(1024)(128)(4,1)}), s8[4194304]{0:T(1024)(128)(4,1)S(1)}, s32[]{:S(2)}) async-start(s8[9437184]{0:T(1024)(128)(4,1)} %bitcast.155), calls=%async_computation.2 | async-start | bytes 8388608 | tf_op jit(solution)/shard_map/while
  225.4 8.2 %slice-start.1 = ((s8[9437184]{0:T(1024)(128)(4,1)}), s8[4194304]{0:T(1024)(128)(4,1)S(1)}, s32[]{:S(2)}) async-start(s8[9437184]{0:T(1024)(128)(4,1)} %bitcast.155), calls=%async_computation.3 | async-start | bytes 8388608 | tf_op jit(solution)/shard_map/while
  225.4 8.2 %slice-start.2 = ((s8[9437184]{0:T(1024)(128)(4,1)}), s8[1048576]{0:T(1024)(128)(4,1)S(1)}, s32[]{:S(2)}) async-start(s8[9437184]{0:T(1024)(128)(4,1)} %bitcast.155), calls=%async_computation.4 | async-start | bytes 2097152 | tf_op jit(solution)/shard_map/while
  225.4 8.2 %copy-start.3 = (s32[4608]{0:T(1024)S(1)}, s32[4608]{0:T(1024)}, u32[]{:S(2)}) copy-start(s32[4608]{0:T(1024)} %get-tuple-element.197) | copy-start | bytes 55300 | tf_op jit(solution)/shard_map/while
  237.3 1.9 copy-start.5
